TPU v7x, 32 devices: a whole 2x2x4 slice. The times are simulated.
32 devices in a mesh: section: 4 (over x, core), row: 4 (over z), col: 2 (over y).
Axes of the slice: x: 2, y: 2, z: 4, core: 2. Of those that a mesh axis runs over, the one named last changes fastest.
Arguments:
- frames: bfloat16 [3, 64, 64, 128], P(None, 'row', 'col'), may hold values from -6 to 6
- gate_weight: bfloat16 [4, 9, 256, 512], P('section'), may hold values from -0.16666667 to 0.16666667
- gate_bias: float32 [4, 512], P('section'), may hold values from -4 to 4
Outputs:
- hidden_final: bfloat16 [4, 64, 64, 128], P('section', 'row', 'col')
- cell_final: float32 [4, 64, 64, 128], P('section', 'row', 'col')
All inputs are finite; a program needn't handle non-finite values.
Results may differ from a plain program's by a relative error of at most 0.0033.
Values may be sent and summed in bfloat16 or wider, within the bound.
A program may use at most 64 MiB of HBM per device.

v0:
```python
import jax
import jax.numpy as jnp
from jax import lax
from jax.experimental import pallas as pl
from jax.experimental.pallas import tpu as pltpu
from jax.sharding import PartitionSpec as P

MESH = pl.DeviceIdType.MESH
DIRS = [(dr, dc) for dr in (-1, 0, 1) for dc in (-1, 0, 1) if (dr, dc) != (0, 0)]
SIDE = 8
CHUNK = 6


def sigmoid(v):
    return 0.5 * jnp.tanh(0.5 * v) + 0.5


def slot(dr, dc):
    return (dr + 1) * 3 + (dc + 1)


def body(sizes, frames, weight, bias, kept_out, added_out, gate_out,
         xc, xe, hc, col_x, col_h, w, ax, ah, acc, cell_mem,
         local_sem, send_sem, xrecv):
    nsec, nrow, ncol = sizes
    steps, rows, cols, width = frames.shape
    pad = steps
    wide = cols + 2 * SIDE
    sec, row, col = lax.axis_index("section"), lax.axis_index("row"), lax.axis_index("col")

    def load_frame(t):
        return pltpu.make_async_copy(frames.at[t], xc.at[t, pl.ds(pad, rows)], local_sem.at[t])

    load_w = pltpu.make_async_copy(weight.at[0], w, local_sem.at[steps])

    @pl.when(sec == 0)
    def _():
        for t in range(steps):
            load_frame(t).start()

    load_w.start()

    def there(dr, dc):
        ok = sec >= 0
        if dr:
            ok = (row > 0) if dr < 0 else (row < nrow - 1)
        if dc:
            okc = (col > 0) if dc < 0 else (col < ncol - 1)
            ok = jnp.logical_and(ok, okc) if dr else okc
        return ok

    def device(ds, dr, dc):
        return {"section": sec + ds, "row": row + dr, "col": col + dc}

    barrier = pltpu.get_barrier_semaphore()

    for t in range(steps):
        xc[t, 0:pad] = jnp.zeros((pad, cols, width), jnp.bfloat16)
        xc[t, pad + rows:] = jnp.zeros((pad, cols, width), jnp.bfloat16)
        xe[t] = jnp.zeros(xe.shape[1:], jnp.bfloat16)

    for ds in (-1, 0, 1):
        okd = (sec > 0) if ds < 0 else (sec < nsec - 1) if ds > 0 else (sec == 0)
        for dr, dc in [(0, 0)] + DIRS:
            if ds == 0 and (dr, dc) == (0, 0):
                continue

            @pl.when(jnp.logical_and(there(dr, dc), okd))
            def _(ds=ds, dr=dr, dc=dc):
                pl.semaphore_signal(barrier, inc=1, device_id=device(ds, dr, dc), device_id_type=MESH)

    def extent(pos, count):
        return 1 + jnp.where(pos > 0, 1, 0) + jnp.where(pos < count - 1, 1, 0)

    near = extent(row, nrow) * extent(col, ncol)
    pl.semaphore_wait(barrier, (extent(sec, nsec) - 1) * near + jnp.where(sec == 0, near - 1, 0))

    def halo_copy(center, base, colbuf, t, kind, ds, dr, dc):
        reach = steps - t
        if dr == 0:
            mine, theirs = pl.ds(0, rows), pl.ds(pad, rows)
        elif dr < 0:
            mine, theirs = pl.ds(0, reach), pl.ds(pad + rows, reach)
        else:
            mine, theirs = pl.ds(rows - reach, reach), pl.ds(pad - reach, reach)
        if dc == 0:
            src = center.at[t, pl.ds(base + (rows - reach if dr > 0 else 0), reach)]
            dst = xc.at[t, theirs]
        else:
            src = colbuf.at[t, 1 if dc > 0 else 0, mine]
            dst = xe.at[t, 0 if dc > 0 else 1, theirs]
        return pltpu.make_async_remote_copy(
            src_ref=src, dst_ref=dst,
            send_sem=send_sem.at[t, kind, slot(dr, dc)],
            recv_sem=xrecv.at[t, slot(-dr, -dc)],
            device_id=device(ds, dr, dc), device_id_type=MESH,
        )

    def halo_sends(act, center, base, colbuf, t, kind, ds):
        for dr, dc in sorted(DIRS, key=lambda d: -abs(d[0]) - abs(d[1])):
            @pl.when(there(dr, dc))
            def _(dr=dr, dc=dc):
                copy = halo_copy(center, base, colbuf, t, kind, ds, dr, dc)
                copy.start() if act == "start" else copy.wait_send()

    def halo_waits(t):
        reach = steps - t
        for dr, dc in DIRS:
            @pl.when(there(dr, dc))
            def _(dr=dr, dc=dc):
                mine = pl.ds(pad, rows) if dr == 0 else pl.ds(pad - reach if dr < 0 else pad + rows, reach)
                dst = xc.at[t, mine] if dc == 0 else xe.at[t, 0 if dc < 0 else 1, mine]
                pltpu.make_async_remote_copy(
                    src_ref=dst, dst_ref=dst,
                    send_sem=send_sem.at[t, 0, slot(0, 0)],
                    recv_sem=xrecv.at[t, slot(dr, dc)],
                    device_id=device(0, dr, dc), device_id_type=MESH,
                ).wait_recv()

    def center_copy(t):
        return pltpu.make_async_remote_copy(
            src_ref=hc.at[t], dst_ref=xc.at[t, pl.ds(pad, rows)],
            send_sem=send_sem.at[t, 0, slot(0, 0)], recv_sem=xrecv.at[t, slot(0, 0)],
            device_id=device(1, 0, 0), device_id_type=MESH,
        )

    @pl.when(sec == 0)
    def _():
        for t in range(steps):
            load_frame(t).wait()
            value = xc[t, pad:pad + rows].astype(jnp.float32)
            col_x[t, 0] = value[:, :SIDE].astype(jnp.bfloat16)
            col_x[t, 1] = value[:, cols - SIDE:].astype(jnp.bfloat16)
            halo_sends("start", xc, pad, col_x, t, 1, 0)

    place = lax.broadcasted_iota(jnp.int32, (wide, width), 0)
    left = jnp.where(col > 0, 1.0, 0.0)
    right = jnp.where(col < ncol - 1, 1.0, 0.0)
    inside = jnp.where(place < SIDE, left, jnp.where(place >= SIDE + cols, right, 1.0))
    above = jnp.where(row > 0, 1.0, 0.0)
    below = jnp.where(row < nrow - 1, 1.0, 0.0)

    def put(out, r, line, full):
        shifted = [pltpu.roll(line, 1, 0), line, pltpu.roll(line, wide - 1, 0)]
        for k, v in enumerate(shifted):
            v = v if full else v[SIDE:SIDE + cols]
            out[r, 0:v.shape[0], k * width:(k + 1) * width] = v.astype(jnp.bfloat16)

    def patches(a, first, count, span):
        return jnp.concatenate(
            [a[first + k:first + k + count, 0:span].reshape(count * span, 3 * width) for k in (-1, 0, 1)], axis=-1
        )

    def kernel_of(half):
        return w[:, half * width:(half + 1) * width, :].reshape(9 * width, 4 * width)

    for t in range(steps):
        e = steps - 1 - t
        full = t < steps - 1
        span = wide if full else cols
        first, last = pad - e, pad + rows + e
        total = (last - first) * span
        if t > 0:
            acc[0:total] = jnp.dot(patches(ah, first, last - first, span), kernel_of(1),
                                   preferred_element_type=jnp.float32)

        @pl.when(sec > 0)
        def _(t=t):
            center = xc.at[t, pl.ds(pad, rows)]
            pltpu.make_async_remote_copy(
                src_ref=center, dst_ref=center, send_sem=send_sem.at[t, 0, slot(0, 0)],
                recv_sem=xrecv.at[t, slot(0, 0)], device_id=device(-1, 0, 0), device_id_type=MESH,
            ).wait_recv()

        halo_waits(t)
        for r in range(first - 1, last + 1):
            line = jnp.concatenate([v.astype(jnp.float32) for v in (xe[t, 0, r], xc[t, r], xe[t, 1, r])], axis=0)
            put(ax, r, line, full)
        if t == 0:
            load_w.wait()
        for r in range(first, last, CHUNK):
            count = min(CHUNK, last - r)
            at = (r - first) * span
            pre = jnp.dot(patches(ax, r, count, span), kernel_of(0), preferred_element_type=jnp.float32)
            pre = pre + bias[...]
            if t > 0:
                pre = pre + acc[at:at + count * span]
            added = sigmoid(pre[:, :width]) * jnp.tanh(pre[:, 2 * width:3 * width])
            added = added.reshape(count, span, width)
            cell = added
            if t > 0:
                old = cell_mem[r:r + count]
                old = old if full else old[:, SIDE:SIDE + cols]
                kept = sigmoid(pre[:, width:2 * width]).reshape(count, span, width) * old
                cell = kept + added
            opened = sigmoid(pre[:, 3 * width:]).reshape(count, span, width)
            hidden = opened * jnp.tanh(cell)
            if full:
                cell_mem[r:r + count] = cell
            else:
                kept_out[0, r - pad:r - pad + count] = kept
                added_out[0, r - pad:r - pad + count] = added
                gate_out[0, r - pad:r - pad + count] = opened
            for q in range(r, r + count):
                line = hidden[q - r]
                core = line[SIDE:SIDE + cols] if full else line
                if pad <= q < pad + rows:
                    hc[t, q - pad] = core.astype(jnp.bfloat16)
                    col_h[t, 0, q - pad] = core[:SIDE].astype(jnp.bfloat16)
                    col_h[t, 1, q - pad] = core[cols - SIDE:].astype(jnp.bfloat16)
                if full:
                    line = line * inside
                    line = line * above if q < pad else line * below if q >= pad + rows else line
                    put(ah, q, line, t + 1 < steps - 1)

        @pl.when(sec < nsec - 1)
        def _(t=t):
            halo_sends("start", hc, 0, col_h, t, 0, 1)
            center_copy(t).start()

    @pl.when(sec == 0)
    def _():
        for t in range(steps):
            halo_sends("wait", xc, pad, col_x, t, 1, 0)

    @pl.when(sec < nsec - 1)
    def _():
        for t in range(steps):
            center_copy(t).wait_send()
            halo_sends("wait", hc, 0, col_h, t, 0, 1)


def solution(mesh):
    sizes = (mesh.shape["section"], mesh.shape["row"], mesh.shape["col"])

    def step(frames, weight, bias):
        steps, rows, cols, width = frames.shape
        high, wide = rows + 2 * steps, cols + 2 * SIDE
        vmem = pl.BlockSpec(memory_space=pltpu.VMEM)
        hbm = pl.BlockSpec(memory_space=pl.ANY)
        bf16 = jnp.bfloat16
        kept, added, opened = pl.pallas_call(
            lambda *refs: body(sizes, *refs),
            out_shape=(jax.ShapeDtypeStruct((1, rows, cols, width), jnp.float32),) * 3,
            in_specs=[hbm, hbm, vmem],
            out_specs=(vmem, vmem, vmem),
            scratch_shapes=[
                pltpu.VMEM((steps, high, cols, width), bf16),
                pltpu.VMEM((steps, 2, high, SIDE, width), bf16),
                pltpu.VMEM((steps, rows, cols, width), bf16),
                pltpu.VMEM((steps, 2, rows, SIDE, width), bf16),
                pltpu.VMEM((steps, 2, rows, SIDE, width), bf16),
                pltpu.VMEM(weight.shape[1:], bf16),
                pltpu.VMEM((high, wide, 3 * width), bf16),
                pltpu.VMEM((high, wide, 3 * width), bf16),
                pltpu.VMEM((high * wide, 4 * width), jnp.float32),
                pltpu.VMEM((high, wide, width), jnp.float32),
                pltpu.SemaphoreType.DMA((steps + 1,)),
                pltpu.SemaphoreType.DMA((steps, 2, 9)),
                pltpu.SemaphoreType.DMA((steps, 9)),
            ],
            compiler_params=pltpu.CompilerParams(collective_id=0, has_side_effects=True),
        )(frames, weight, bias)
        cell = kept + added
        return (opened * jnp.tanh(cell)).astype(bf16), cell

    return jax.shard_map(
        step,
        mesh=mesh,
        in_specs=(P(None, "row", "col", None), P("section", None, None, None), P("section", None)),
        out_specs=(P("section", "row", "col", None), P("section", "row", "col", None)),
        check_vma=False,
    )
```

profile of v0, /device:TPU:11, one launch (start us, length us, event | category | flops | bytes accessed | tf_op | source)
XLA Modules:
  0.0 32.6 jit_solution(12533277966527583710)
XLA Ops:
  0.6 30.1 %shard_map.50 = (f32[1,16,32,128]{3,2,1,0:T(8,128)}, f32[1,16,32,128]{3,2,1,0:T(8,128)}, f32[1,16,32,128]{3,2,1,0:T(8,128)}) custom-call(bf16[3,16,32,128]{3,2,1,0:T(8,128)(2,1)} %refs_0_.1, bf16[1,9,256,512]{3,2,1,0:T(8,128)(2,1)} %refs_1_.1, f32[1,512]{1,0:T(1,128)} %refs_2_.1), custom_call_target="tpu_custom_call" | custom-call | tf_op jit(solution)/shard_map/pallas_call | solution.py:242
  30.7 1.9 %multiply_convert_fusion = (bf16[1,16,32,128]{3,2,1,0:T(8,128)(2,1)}, f32[1,16,32,128]{3,2,1,0:T(8,128)}) fusion(f32[1,16,32,128]{3,2,1,0:T(8,128)} %get-tuple-element.5, f32[1,16,32,128]{3,2,1,0:T(8,128)} %get-tuple-element.6, f32[1,16,32,128]{3,2,1,0:T(8,128)} %get-tuple-element.7), kind=kLoop, calls=%fused_computation | loop fusion | flops 196608 | bytes 1179648 | tf_op jit(solution)/shard_map/convert_element_type | solution.py:265
where the time goes:
time: 33.1 us; the launch traced here: 32.6 us
  Pallas kernels  30.1 us (91%)
  other arithmetic  1.91 us (6%)
  between operations  0.64 us (2%)
    pallas_call x1, Pallas kernels, step(): pl.pallas_call(lambda *refs: body(sizes, *refs), out_shape=(jax.ShapeDtyp...  30.1 us
    convert_element_type x1, other arithmetic, step(): return ((opened * jnp.tanh(cell)).astype(bf16), cell)  1.91 us

commit v1 on v0

--- a/solution.py
+++ b/solution.py
@@ -237,7 +237,7 @@
         steps, rows, cols, width = frames.shape
         high, wide = rows + 2 * steps, cols + 2 * SIDE
         vmem = pl.BlockSpec(memory_space=pltpu.VMEM)
-        hbm = pl.BlockSpec(memory_space=pl.ANY)
+        hbm = pl.BlockSpec(memory_space=pltpu.HBM)
         bf16 = jnp.bfloat16
         kept, added, opened = pl.pallas_call(
             lambda *refs: body(sizes, *refs),
@@ -259,8 +259,8 @@
                 pltpu.SemaphoreType.DMA((steps, 2, 9)),
                 pltpu.SemaphoreType.DMA((steps, 9)),
             ],
-            compiler_params=pltpu.CompilerParams(collective_id=0, has_side_effects=True),
-        )(frames, weight, bias)
+            compiler_params=pltpu.CompilerParams(collective_id=0, has_side_effects=True, vmem_limit_bytes=20<<20),
+        )(*[pltpu.with_memory_space_constraint(v, pltpu.HBM) for v in (frames, weight, bias)])
         cell = kept + added
         return (opened * jnp.tanh(cell)).astype(bf16), cell
 

time: 33.1 us -> 31.1 us (0.940)
  other arithmetic: 1.91 us -> 0.8 us
  Pallas kernels: 30.1 us -> 29.2 us
    convert_element_type x1, other arithmetic: 1.91 us -> 0.8 us  [step(): return ((opened * jnp.tanh(cell)).astype(bf16), cell)]
    pallas_call x1, Pallas kernels: 30.1 us -> 29.2 us  [step(): pl.pallas_call(lambda *refs: body(sizes, *refs), out_shape=(jax.ShapeDtyp...]
where the time goes in v1:
time: 31.1 us; the launch traced here: 30.6 us
  Pallas kernels  29.2 us (94%)
  other arithmetic  0.8 us (3%)
  between operations  0.64 us (2%)
    pallas_call x1, Pallas kernels, step(): pl.pallas_call(lambda *refs: body(sizes, *refs), out_shape=(jax.ShapeDtyp...  29.2 us
    convert_element_type x1, other arithmetic, step(): return ((opened * jnp.tanh(cell)).astype(bf16), cell)  0.8 us

profile of v1, /device:TPU:11, one launch (start us, length us, event | category | flops | bytes accessed | tf_op | source)
XLA Modules:
  0.0 30.6 jit_solution(221910850258640837)
XLA Ops:
  0.6 29.2 %shard_map.50 = (f32[1,16,32,128]{3,2,1,0:T(8,128)S(1)}, f32[1,16,32,128]{3,2,1,0:T(8,128)S(1)}, f32[1,16,32,128]{3,2,1,0:T(8,128)S(1)}) custom-call(bf16[3,16,32,128]{3,2,1,0:T(8,128)(2,1)} %refs_0_.1, bf16[1,9,256,512]{3,2,1,0:T(8,128)(2,1)} %refs_1_.1, f32[1,512]{1,0:T(1,128)} %refs_2_.1), custom_call_target="tpu_custom_call" | custom-call | tf_op jit(solution)/shard_map/pallas_call | solution.py:242
  29.8 0.8 %multiply_convert_fusion = (bf16[1,16,32,128]{3,2,1,0:T(8,128)(2,1)}, f32[1,16,32,128]{3,2,1,0:T(8,128)}) fusion(f32[1,16,32,128]{3,2,1,0:T(8,128)S(1)} %get-tuple-element.5, f32[1,16,32,128]{3,2,1,0:T(8,128)S(1)} %get-tuple-element.6, f32[1,16,32,128]{3,2,1,0:T(8,128)S(1)} %get-tuple-element.7), kind=kLoop, calls=%fused_computation | loop fusion | flops 196608 | bytes 1179648 | tf_op jit(solution)/shard_map/convert_element_type | solution.py:265

commit v2 on v1

v2 whole, which is shorter than its diff:
```python
import jax
import jax.numpy as jnp
from jax import lax
from jax.experimental import pallas as pl
from jax.experimental.pallas import tpu as pltpu
from jax.sharding import PartitionSpec as P

MESH = pl.DeviceIdType.MESH
DIRS = [(dr, dc) for dr in (-1, 0, 1) for dc in (-1, 0, 1) if (dr, dc) != (0, 0)]
RING = 8
MSGS = 15


def sigmoid(v):
    return 0.5 * jnp.tanh(0.5 * v) + 0.5


def body(sizes, frames, weight, bias_in, kept_out, added_out, gate_out,
         xc, xe, hc, hr, col_h, w, bias, sx, rx, sh, rh, acc, cell_c, cell_r,
         local_sem, frame_sem, send_sem, recv_sem):
    nsec, nrow, ncol = sizes
    steps, rows, cols, width = frames.shape
    pad = steps + 1
    wide = cols + RING
    bf16 = jnp.bfloat16
    f32 = jnp.float32
    sec, row, col = lax.axis_index("section"), lax.axis_index("row"), lax.axis_index("col")

    def there(dr, dc):
        ok = sec >= 0
        if dr:
            ok = (row > 0) if dr < 0 else (row < nrow - 1)
        if dc:
            okc = (col > 0) if dc < 0 else (col < ncol - 1)
            ok = jnp.logical_and(ok, okc) if dr else okc
        return ok

    def device(ds, dr, dc):
        return {"section": sec + ds, "row": row + dr, "col": col + dc}

    def load_frame(t):
        return pltpu.make_async_copy(frames.at[t], xc.at[t, pl.ds(pad, rows)], local_sem.at[t])

    def load_w(half):
        part = pl.ds(half * width, width)
        return pltpu.make_async_copy(weight.at[0, :, part], w.at[:, part], local_sem.at[steps + half])

    load_b = pltpu.make_async_copy(bias_in, bias, local_sem.at[steps + 2])

    def direct(s):
        return s % 2 == 0

    def extra(s, t):
        return steps - t - s % 2

    def edge(s):
        return nsec + 1 - s

    def rng(a, b):
        return pl.ds(pad + a, b - a)

    def halo(t, reach, dr, dc):
        if dr == 0:
            return (0, rows), (0, rows)
        if dr < 0:
            return (0, reach), (rows, rows + reach)
        return (rows - reach, rows), (-reach, 0)

    def frame_msgs(t):
        reach = pad - t
        out = []
        for dr, dc in sorted(DIRS, key=lambda d: -abs(d[0]) - abs(d[1])):
            mine, theirs = halo(t, reach, dr, dc)
            src = frames.at[t, pl.ds(mine[0], mine[1] - mine[0])]
            if dc == 0:
                dst = xc.at[t, rng(*theirs)]
            else:
                src = frames.at[t, pl.ds(mine[0], mine[1] - mine[0]), pl.ds(0 if dc < 0 else cols - RING, RING)]
                dst = xe.at[t, 1 if dc < 0 else 0, rng(*theirs)]
            out.append((dr, dc, src, dst, 3 * (dr + 1) + dc + 1))
        return out

    def exchange_msgs(s, t, phase):
        reach, q = pad - t, edge(s)
        out = []

        def side(dc, mine, theirs, k, dr=0):
            src = col_h.at[t, 0 if dc < 0 else 1, pl.ds(mine[0], mine[1] - mine[0])]
            dst = xe.at[t, 1 if dc < 0 else 0, rng(*theirs)]
            out.append((dr, dc, src, dst, k))

        def middle(mine, theirs, k, dr=0):
            out.append((dr, 0, hc.at[t, rng(*mine)], xc.at[t, rng(*theirs)], k))

        if phase == 0:
            for k, (dr, dc) in enumerate([d for d in DIRS if d[0] and d[1]]):
                mine, theirs = halo(t, reach, dr, dc)
                side(dc, mine, theirs, 8 + k, dr)
            for k, dr in enumerate((-1, 1)):
                mine, theirs = halo(t, reach, dr, 0)
                middle(mine, theirs, 2 + k, dr)
            for k, span in enumerate(((0, q), (rows - q, rows))):
                for j, dc in enumerate((-1, 1)):
                    side(dc, span, span, 4 + 2 * j + k)
            for k, span in enumerate(((0, q), (rows - q, rows))):
                middle(span, span, k)
        else:
            span = (q, rows - q)
            for j, dc in enumerate((-1, 1)):
                side(dc, span, span, 13 + j)
            middle(span, span, 12)
        return out

    def direct_msgs(s, t, phase):
        e, q = extra(s, t), edge(s)
        spans = ((-e, q), (rows - q, rows + e)) if phase == 0 else ((q, rows - q),)
        out = []
        for k, span in enumerate(spans):
            at = rng(*span)
            out.append((0, 0, hc.at[t, at], xc.at[t, at], 6 * phase + 2 * k))
            out.append((0, 0, hr.at[t, at], xe.at[t, 0, at], 6 * phase + 2 * k + 1))
        return out

    def msgs(s, t, phase):
        return direct_msgs(s, t, phase) if direct(s) else exchange_msgs(s, t, phase)

    def each(items, ds, t, sem, act):
        for dr, dc, src, dst, k in items:
            def go(dr=dr, dc=dc, src=src, dst=dst, k=k):
                if act == "recv":
                    pltpu.make_async_remote_copy(
                        src_ref=dst, dst_ref=dst, send_sem=sem.at[t, k], recv_sem=recv_sem.at[t, k],
                        device_id=device(-ds, -dr, -dc), device_id_type=MESH,
                    ).wait_recv()
                    return
                copy = pltpu.make_async_remote_copy(
                    src_ref=src, dst_ref=dst, send_sem=sem.at[t, k], recv_sem=recv_sem.at[t, k],
                    device_id=device(ds, dr, dc), device_id_type=MESH,
                )
                copy.start() if act == "start" else copy.wait_send()
            if (dr, dc) == (0, 0):
                go()
            else:
                pl.when(there(-dr, -dc) if act == "recv" else there(dr, dc))(go)

    barrier = pltpu.get_barrier_semaphore()

    def signal(ds, dr, dc):
        def go():
            pl.semaphore_signal(barrier, inc=1, device_id=device(ds, dr, dc), device_id_type=MESH)
        if (dr, dc) == (0, 0):
            go()
        else:
            pl.when(there(dr, dc))(go)

    def extent(pos, count):
        return 1 + jnp.where(pos > 0, 1, 0) + jnp.where(pos < count - 1, 1, 0)

    near = extent(row, nrow) * extent(col, ncol)

    place = lax.broadcasted_iota(jnp.int32, (RING, width), 0)
    left = jnp.where(col > 0, 1.0, 0.0)
    right = jnp.where(col < ncol - 1, 1.0, 0.0)
    inside = jnp.where(place < RING // 2, right, left)
    above = jnp.where(row > 0, 1.0, 0.0)
    below = jnp.where(row < nrow - 1, 1.0, 0.0)

    def spread(shift, ring, r, line):
        back, ahead = pltpu.roll(line, 1, 0), pltpu.roll(line, wide - 1, 0)
        shift[r + pad, :, 0:width] = back[:cols].astype(bf16)
        shift[r + pad, :, width:] = ahead[:cols].astype(bf16)
        for k, v in enumerate((back, line, ahead)):
            ring[(r + pad) * RING:(r + pad + 1) * RING, k * width:(k + 1) * width] = v[cols:]

    def taps(center, shift, ring, pieces, has_ring, which):
        blocks = []
        for k in which:
            dr, dc = k // 3 - 1, k % 3 - 1
            parts = []
            for r0, n in pieces:
                at = slice(r0 + dr + pad, r0 + dr + pad + n)
                v = center[at] if dc == 0 else shift[at, :, 0:width] if dc < 0 else shift[at, :, width:]
                parts.append(v.reshape(n * cols, width))
            if has_ring:
                lines = [ring[(r0 + dr + pad) * RING:(r0 + dr + pad + n) * RING, (dc + 1) * width:(dc + 2) * width]
                         for r0, n in pieces]
                parts.append((jnp.concatenate(lines, axis=0) if len(lines) > 1 else lines[0]).astype(bf16))
            blocks.append(jnp.concatenate(parts, axis=0) if len(parts) > 1 else parts[0])
        return blocks

    def kernel_of(half, which):
        return [w[k, half * width:(half + 1) * width, :] for k in which]

    def dot(a, b):
        return jnp.dot(jnp.concatenate(a, axis=1), jnp.concatenate(b, axis=0), preferred_element_type=f32)

    every = list(range(9))

    def section(s):
        last_sec = s == nsec - 1
        q = edge(s)

        load_w(0).start()
        load_b.start()
        load_w(1).start()
        if s == 0:
            for t in range(steps):
                load_frame(t).start()
        if direct(s):
            for t in range(steps):
                xc[t, 0:pad] = jnp.zeros((pad, cols, width), bf16)
                xc[t, pad + rows:] = jnp.zeros((pad, cols, width), bf16)
                xe[t] = jnp.zeros(xe.shape[1:], bf16)
        if s == 0:
            for dr, dc in DIRS:
                signal(0, dr, dc)
        elif direct(s - 1):
            signal(-1, 0, 0)
        else:
            for dr, dc in [(0, 0)] + DIRS:
                signal(-1, dr, dc)
        wanted = 0
        if s == 0:
            wanted = near - 1
        if not last_sec:
            wanted = wanted + (1 if direct(s) else near)
        if s == 0 or not last_sec:
            pl.semaphore_wait(barrier, wanted)
        if s == 0:
            for t in range(steps):
                each(frame_msgs(t), 0, t, frame_sem, "start")

        for t in range(steps):
            e = extra(s, t)
            has_ring = e > 0
            span = wide if has_ring else cols
            final = t == steps - 1
            chunks = [[(-e, q + e), (rows - q, q + e)], [(q, rows - 2 * q)]]
            fresh = [[(-e - 1, q + 1), (rows - q - 1, rows + e + 1)], [(q + 1, rows - q - 1)]]
            sizes_m = [sum(n for _, n in c) * span for c in chunks]
            starts = [0, sizes_m[0]]
            if t > 0:
                if t == 1:
                    load_w(1).wait()
                if s > 0:
                    for c in range(2):
                        acc[starts[c]:starts[c] + sizes_m[c]] = dot(
                            taps(hc.at[t - 1], sh.at[t - 1], rh.at[t - 1], chunks[c], has_ring, every[:8]),
                            kernel_of(1, every[:8]))
            for c in range(2):
                pieces = chunks[c]
                if s > 0:
                    each(msgs(s - 1, t, c), 1, t, send_sem, "recv")
                elif c == 0:
                    load_frame(t).wait()
                    each(frame_msgs(t), 0, t, frame_sem, "recv")
                for lo, hi in fresh[c]:
                    for r in range(lo, hi):
                        if direct(s):
                            ring = jnp.where(place < RING // 2, xe[t, 1, r + pad].astype(f32), xe[t, 0, r + pad].astype(f32))
                        else:
                            ring = xe[t, 0, r + pad].astype(f32)
                        spread(sx, rx, r, jnp.concatenate([xc[t, r + pad].astype(f32), ring], axis=0))
                if t == 0 and c == 0:
                    load_w(0).wait()
                    load_b.wait()
                a = taps(xc.at[t], sx, rx, pieces, has_ring, every)
                b = kernel_of(0, every)
                if t > 0:
                    which = every if s == 0 else every[8:]
                    a = a + taps(hc.at[t - 1], sh.at[t - 1], rh.at[t - 1], pieces, has_ring, which)
                    b = b + kernel_of(1, which)
                pre = dot(a, b) + bias[...]
                if t > 0 and s > 0:
                    pre = pre + acc[starts[c]:starts[c] + sizes_m[c]]
                total = sum(n for _, n in pieces)
                at_core, at_ring = 0, total * cols
                for r0, n in pieces:
                    groups = [(cols, at_core, cell_c)] + ([(RING, at_ring, cell_r)] if has_ring else [])
                    made = []
                    for span_g, at, mem in groups:
                        p = pre[at:at + n * span_g]
                        shape = (n, span_g, width)
                        added = (sigmoid(p[:, :width]) * jnp.tanh(p[:, 2 * width:3 * width])).reshape(shape)
                        cell = added
                        if t > 0:
                            kept = sigmoid(p[:, width:2 * width]).reshape(shape) * mem[r0 + pad:r0 + pad + n]
                            cell = kept + added
                        opened = sigmoid(p[:, 3 * width:]).reshape(shape)
                        if not final:
                            mem[r0 + pad:r0 + pad + n] = cell
                        elif span_g == cols:
                            lo, hi = max(r0, 0), min(r0 + n, rows)
                            kept_out[0, lo:hi] = kept[lo - r0:hi - r0]
                            added_out[0, lo:hi] = added[lo - r0:hi - r0]
                            gate_out[0, lo:hi] = opened[lo - r0:hi - r0]
                        made.append(opened * jnp.tanh(cell))
                    at_core, at_ring = at_core + n * cols, at_ring + n * RING
                    if final and last_sec:
                        continue
                    for r in range(r0, r0 + n):
                        core = made[0][r - r0]
                        if has_ring:
                            ring = made[1][r - r0] * inside
                        if r < 0:
                            core, ring = core * above, ring * above
                        elif r >= rows:
                            core, ring = core * below, ring * below
                        hc[t, r + pad] = core.astype(bf16)
                        if not last_sec:
                            if direct(s):
                                hr[t, r + pad] = ring.astype(bf16)
                            elif 0 <= r < rows:
                                col_h[t, 0, r] = core[:RING].astype(bf16)
                                col_h[t, 1, r] = core[cols - RING:].astype(bf16)
                        if not final:
                            spread(sh.at[t], rh.at[t], r, jnp.concatenate([core, ring], axis=0))
                if not last_sec:
                    each(msgs(s, t, c), 1, t, send_sem, "start")

        if s == 0:
            for t in range(steps):
                each(frame_msgs(t), 0, t, frame_sem, "wait")
        if steps == 1:
            load_w(1).wait()
        if not last_sec:
            for t in range(steps):
                for c in range(2):
                    each(msgs(s, t, c), 1, t, send_sem, "wait")

    for s in range(nsec):
        @pl.when(sec == s)
        def _(s=s):
            section(s)


def solution(mesh):
    sizes = (mesh.shape["section"], mesh.shape["row"], mesh.shape["col"])

    def step(frames, weight, bias):
        steps, rows, cols, width = frames.shape
        pad = steps + 1
        assert pad <= RING // 2 and 2 * (sizes[0] + 1) < rows
        high = rows + 2 * pad
        vmem = pl.BlockSpec(memory_space=pltpu.VMEM)
        hbm = pl.BlockSpec(memory_space=pl.ANY)
        bf16, f32 = jnp.bfloat16, jnp.float32
        kept, added, opened = pl.pallas_call(
            lambda *refs: body(sizes, *refs),
            out_shape=(jax.ShapeDtypeStruct((1, rows, cols, width), f32),) * 3,
            in_specs=[hbm, hbm, hbm],
            out_specs=(vmem, vmem, vmem),
            scratch_shapes=[
                pltpu.VMEM((steps, high, cols, width), bf16),
                pltpu.VMEM((steps, 2, high, RING, width), bf16),
                pltpu.VMEM((steps, high, cols, width), bf16),
                pltpu.VMEM((steps, high, RING, width), bf16),
                pltpu.VMEM((steps, 2, rows, RING, width), bf16),
                pltpu.VMEM(weight.shape[1:], bf16),
                pltpu.VMEM(bias.shape, f32),
                pltpu.VMEM((high, cols, 2 * width), bf16),
                pltpu.VMEM((high * RING, 3 * width), f32),
                pltpu.VMEM((steps, high, cols, 2 * width), bf16),
                pltpu.VMEM((steps, high * RING, 3 * width), f32),
                pltpu.VMEM((high * (cols + RING), 4 * width), f32),
                pltpu.VMEM((high, cols, width), f32),
                pltpu.VMEM((high, RING, width), f32),
                pltpu.SemaphoreType.DMA((steps + 3,)),
                pltpu.SemaphoreType.DMA((steps, MSGS)),
                pltpu.SemaphoreType.DMA((steps, MSGS)),
                pltpu.SemaphoreType.DMA((steps, MSGS)),
            ],
            compiler_params=pltpu.CompilerParams(
                collective_id=0, has_side_effects=True, vmem_limit_bytes=24 << 20),
        )(*[pltpu.with_memory_space_constraint(v, pltpu.HBM) for v in (frames, weight, bias)])
        cell = kept + added
        return (opened * jnp.tanh(cell)).astype(bf16), cell

    return jax.shard_map(
        step,
        mesh=mesh,
        in_specs=(P(None, "row", "col", None), P("section", None, None, None), P("section", None)),
        out_specs=(P("section", "row", "col", None), P("section", "row", "col", None)),
        check_vma=False,
    )
```

time: 31.1 us -> 25.4 us (0.82)
  Pallas kernels: 29.2 us -> 23.8 us
    pallas_call x1, Pallas kernels: 29.2 us -> 23.8 us  [step(): pl.pallas_call(lambda *refs: body(sizes, *refs), out_shape=(jax.ShapeDtyp...]
where the time goes in v2:
time: 25.4 us; the launch traced here: 25.2 us
  Pallas kernels  23.8 us (94%)
  other arithmetic  0.8 us (3%)
  between operations  0.64 us (3%)
    pallas_call x1, Pallas kernels, step(): pl.pallas_call(lambda *refs: body(sizes, *refs), out_shape=(jax.ShapeDtyp...  23.8 us
    convert_element_type x1, other arithmetic, step(): return ((opened * jnp.tanh(cell)).astype(bf16), cell)  0.8 us

profile of v2, /device:TPU:11, one launch (start us, length us, event | category | flops | bytes accessed | tf_op | source)
XLA Modules:
  0.0 25.2 jit_solution(8330341250379494731)
XLA Ops:
  0.6 23.8 %shard_map.50 = (f32[1,16,32,128]{3,2,1,0:T(8,128)S(1)}, f32[1,16,32,128]{3,2,1,0:T(8,128)S(1)}, f32[1,16,32,128]{3,2,1,0:T(8,128)S(1)}) custom-call(bf16[3,16,32,128]{3,2,1,0:T(8,128)(2,1)} %refs_0_.1, bf16[1,9,256,512]{3,2,1,0:T(8,128)(2,1)} %refs_1_.1, f32[1,512]{1,0:T(1,128)} %refs_2_.1), custom_call_target="tpu_custom_call" | custom-call | tf_op jit(solution)/shard_map/pallas_call | solution.py:348
  24.4 0.8 %multiply_convert_fusion = (bf16[1,16,32,128]{3,2,1,0:T(8,128)(2,1)}, f32[1,16,32,128]{3,2,1,0:T(8,128)}) fusion(f32[1,16,32,128]{3,2,1,0:T(8,128)S(1)} %get-tuple-element.5, f32[1,16,32,128]{3,2,1,0:T(8,128)S(1)} %get-tuple-element.6, f32[1,16,32,128]{3,2,1,0:T(8,128)S(1)} %get-tuple-element.7), kind=kLoop, calls=%fused_computation | loop fusion | flops 196608 | bytes 1179648 | tf_op jit(solution)/shard_map/convert_element_type | solution.py:377

commit v3 on v2

--- a/solution.py
+++ b/solution.py
@@ -16,7 +16,7 @@
 
 
 def body(sizes, frames, weight, bias_in, kept_out, added_out, gate_out,
-         xc, xe, hc, hr, col_h, w, bias, sx, rx, sh, rh, acc, cell_c, cell_r,
+         xc, xe, xn, hc, hr, col_h, col_n, w, bias, sx, rx, sh, rh, acc, cell_c, cell_r,
          local_sem, frame_sem, send_sem, recv_sem):
     nsec, nrow, ncol = sizes
     steps, rows, cols, width = frames.shape
@@ -41,6 +41,10 @@
     def load_frame(t):
         return pltpu.make_async_copy(frames.at[t], xc.at[t, pl.ds(pad, rows)], local_sem.at[t])
 
+    def load_side(t, k):
+        part = pl.ds(0 if k == 0 else cols - RING, RING)
+        return pltpu.make_async_copy(frames.at[t, :, part], col_h.at[t, k], local_sem.at[steps + 3 + 2 * t + k])
+
     def load_w(half):
         part = pl.ds(half * width, width)
         return pltpu.make_async_copy(weight.at[0, :, part], w.at[:, part], local_sem.at[steps + half])
@@ -71,25 +75,29 @@
         out = []
         for dr, dc in sorted(DIRS, key=lambda d: -abs(d[0]) - abs(d[1])):
             mine, theirs = halo(t, reach, dr, dc)
-            src = frames.at[t, pl.ds(mine[0], mine[1] - mine[0])]
             if dc == 0:
+                src = xc.at[t, rng(*mine)]
                 dst = xc.at[t, rng(*theirs)]
             else:
-                src = frames.at[t, pl.ds(mine[0], mine[1] - mine[0]), pl.ds(0 if dc < 0 else cols - RING, RING)]
+                src = col_h.at[t, 0 if dc < 0 else 1, pl.ds(mine[0], mine[1] - mine[0])]
                 dst = xe.at[t, 1 if dc < 0 else 0, rng(*theirs)]
             out.append((dr, dc, src, dst, 3 * (dr + 1) + dc + 1))
         return out
 
-    def exchange_msgs(s, t, phase):
+    def exchange_msgs(s, t, phase, part=None):
         reach, q = pad - t, edge(s)
         out = []
 
         def side(dc, mine, theirs, k, dr=0):
-            src = col_h.at[t, 0 if dc < 0 else 1, pl.ds(mine[0], mine[1] - mine[0])]
-            dst = xe.at[t, 1 if dc < 0 else 0, rng(*theirs)]
+            if part == int(mine[0] == 0):
+                return
+            src = col_n.at[t, 0 if dc < 0 else 1, pl.ds(mine[0], mine[1] - mine[0])]
+            dst = xn.at[t, 1 if dc < 0 else 0, rng(*theirs)]
             out.append((dr, dc, src, dst, k))
 
         def middle(mine, theirs, k, dr=0):
+            if part == int(mine[0] == 0):
+                return
             out.append((dr, 0, hc.at[t, rng(*mine)], xc.at[t, rng(*theirs)], k))
 
         if phase == 0:
@@ -196,21 +204,37 @@
 
     every = list(range(9))
 
+    def waits(s, t, c):
+        if s == nsec - 1:
+            return t == steps - 1 or c == 1
+        return not direct(s) and t == steps - 1 and c == 1
+
+    def send_frame(t):
+        load_side(t, 0).wait()
+        load_side(t, 1).wait()
+        load_frame(t).wait()
+        each(frame_msgs(t), 0, t, frame_sem, "start")
+
     def section(s):
         last_sec = s == nsec - 1
         q = edge(s)
 
+        if s == 0:
+            for t in range(steps):
+                load_side(t, 0).start()
+                load_side(t, 1).start()
+                load_frame(t).start()
         load_w(0).start()
         load_b.start()
         load_w(1).start()
-        if s == 0:
-            for t in range(steps):
-                load_frame(t).start()
         if direct(s):
             for t in range(steps):
                 xc[t, 0:pad] = jnp.zeros((pad, cols, width), bf16)
                 xc[t, pad + rows:] = jnp.zeros((pad, cols, width), bf16)
-                xe[t] = jnp.zeros(xe.shape[1:], bf16)
+                if s == 0:
+                    xe[t] = jnp.zeros(xe.shape[1:], bf16)
+                else:
+                    xn[t] = jnp.zeros(xn.shape[1:], bf16)
         if s == 0:
             for dr, dc in DIRS:
                 signal(0, dr, dc)
@@ -227,8 +251,10 @@
         if s == 0 or not last_sec:
             pl.semaphore_wait(barrier, wanted)
         if s == 0:
-            for t in range(steps):
-                each(frame_msgs(t), 0, t, frame_sem, "start")
+            send_frame(0)
+            each(frame_msgs(0), 0, 0, frame_sem, "wait")
+            if steps > 1:
+                send_frame(1)
 
         for t in range(steps):
             e = extra(s, t)
@@ -237,26 +263,27 @@
             final = t == steps - 1
             chunks = [[(-e, q + e), (rows - q, q + e)], [(q, rows - 2 * q)]]
             fresh = [[(-e - 1, q + 1), (rows - q - 1, rows + e + 1)], [(q + 1, rows - q - 1)]]
-            sizes_m = [sum(n for _, n in c) * span for c in chunks]
-            starts = [0, sizes_m[0]]
-            if t > 0:
-                if t == 1:
-                    load_w(1).wait()
-                if s > 0:
-                    for c in range(2):
-                        acc[starts[c]:starts[c] + sizes_m[c]] = dot(
-                            taps(hc.at[t - 1], sh.at[t - 1], rh.at[t - 1], chunks[c], has_ring, every[:8]),
-                            kernel_of(1, every[:8]))
+            if t == 1:
+                load_w(1).wait()
             for c in range(2):
                 pieces = chunks[c]
+                split = t > 0 and s > 0 and waits(s, t, c)
+                total = sum(n for _, n in pieces)
+                if split:
+                    acc[0:total * span] = dot(
+                        taps(hc.at[t - 1], sh.at[t - 1], rh.at[t - 1], pieces, has_ring, every[:8]),
+                        kernel_of(1, every[:8]))
                 if s > 0:
                     each(msgs(s - 1, t, c), 1, t, send_sem, "recv")
                 elif c == 0:
-                    load_frame(t).wait()
                     each(frame_msgs(t), 0, t, frame_sem, "recv")
+                    if t + 2 < steps:
+                        send_frame(t + 2)
                 for lo, hi in fresh[c]:
                     for r in range(lo, hi):
-                        if direct(s):
+                        if direct(s) and s > 0:
+                            ring = jnp.concatenate([xn[t, 1, r + pad].astype(f32), xn[t, 0, r + pad].astype(f32)], axis=0)
+                        elif direct(s):
                             ring = jnp.where(place < RING // 2, xe[t, 1, r + pad].astype(f32), xe[t, 0, r + pad].astype(f32))
                         else:
                             ring = xe[t, 0, r + pad].astype(f32)
@@ -264,62 +291,65 @@
                 if t == 0 and c == 0:
                     load_w(0).wait()
                     load_b.wait()
-                a = taps(xc.at[t], sx, rx, pieces, has_ring, every)
-                b = kernel_of(0, every)
-                if t > 0:
-                    which = every if s == 0 else every[8:]
-                    a = a + taps(hc.at[t - 1], sh.at[t - 1], rh.at[t - 1], pieces, has_ring, which)
-                    b = b + kernel_of(1, which)
-                pre = dot(a, b) + bias[...]
-                if t > 0 and s > 0:
-                    pre = pre + acc[starts[c]:starts[c] + sizes_m[c]]
-                total = sum(n for _, n in pieces)
-                at_core, at_ring = 0, total * cols
-                for r0, n in pieces:
-                    groups = [(cols, at_core, cell_c)] + ([(RING, at_ring, cell_r)] if has_ring else [])
-                    made = []
-                    for span_g, at, mem in groups:
-                        p = pre[at:at + n * span_g]
-                        shape = (n, span_g, width)
-                        added = (sigmoid(p[:, :width]) * jnp.tanh(p[:, 2 * width:3 * width])).reshape(shape)
-                        cell = added
-                        if t > 0:
-                            kept = sigmoid(p[:, width:2 * width]).reshape(shape) * mem[r0 + pad:r0 + pad + n]
-                            cell = kept + added
-                        opened = sigmoid(p[:, 3 * width:]).reshape(shape)
-                        if not final:
-                            mem[r0 + pad:r0 + pad + n] = cell
-                        elif span_g == cols:
-                            lo, hi = max(r0, 0), min(r0 + n, rows)
-                            kept_out[0, lo:hi] = kept[lo - r0:hi - r0]
-                            added_out[0, lo:hi] = added[lo - r0:hi - r0]
-                            gate_out[0, lo:hi] = opened[lo - r0:hi - r0]
-                        made.append(opened * jnp.tanh(cell))
-                    at_core, at_ring = at_core + n * cols, at_ring + n * RING
-                    if final and last_sec:
-                        continue
-                    for r in range(r0, r0 + n):
-                        core = made[0][r - r0]
-                        if has_ring:
-                            ring = made[1][r - r0] * inside
-                        if r < 0:
-                            core, ring = core * above, ring * above
-                        elif r >= rows:
-                            core, ring = core * below, ring * below
-                        hc[t, r + pad] = core.astype(bf16)
-                        if not last_sec:
-                            if direct(s):
-                                hr[t, r + pad] = ring.astype(bf16)
-                            elif 0 <= r < rows:
-                                col_h[t, 0, r] = core[:RING].astype(bf16)
-                                col_h[t, 1, r] = core[cols - RING:].astype(bf16)
-                        if not final:
-                            spread(sh.at[t], rh.at[t], r, jnp.concatenate([core, ring], axis=0))
-                if not last_sec:
-                    each(msgs(s, t, c), 1, t, send_sem, "start")
+                blocks = [[p] for p in pieces] if c == 0 and not last_sec and not direct(s) else [pieces]
+                for i, part in enumerate(blocks):
+                    a = taps(xc.at[t], sx, rx, part, has_ring, every)
+                    b = kernel_of(0, every)
+                    if t > 0:
+                        which = every[8:] if split else every
+                        a = a + taps(hc.at[t - 1], sh.at[t - 1], rh.at[t - 1], part, has_ring, which)
+                        b = b + kernel_of(1, which)
+                    pre = dot(a, b) + bias[...]
+                    if split:
+                        pre = pre + acc[0:total * span]
+                    at_core, at_ring = 0, sum(n for _, n in part) * cols
+                    for r0, n in part:
+                        groups = [(cols, at_core, cell_c)] + ([(RING, at_ring, cell_r)] if has_ring else [])
+                        made = []
+                        for span_g, at, mem in groups:
+                            p = pre[at:at + n * span_g]
+                            shape = (n, span_g, width)
+                            added = (sigmoid(p[:, :width]) * jnp.tanh(p[:, 2 * width:3 * width])).reshape(shape)
+                            cell = added
+                            if t > 0:
+                                kept = sigmoid(p[:, width:2 * width]).reshape(shape) * mem[r0 + pad:r0 + pad + n]
+                                cell = kept + added
+                            opened = sigmoid(p[:, 3 * width:]).reshape(shape)
+                            if not final:
+                                mem[r0 + pad:r0 + pad + n] = cell
+                            elif span_g == cols:
+                                lo, hi = max(r0, 0), min(r0 + n, rows)
+                                kept_out[0, lo:hi] = kept[lo - r0:hi - r0]
+                                added_out[0, lo:hi] = added[lo - r0:hi - r0]
+                                gate_out[0, lo:hi] = opened[lo - r0:hi - r0]
+                            made.append(opened * jnp.tanh(cell))
+                        at_core, at_ring = at_core + n * cols, at_ring + n * RING
+                        if final and last_sec:
+                            continue
+                        for r in range(r0, r0 + n):
+                            core = made[0][r - r0]
+                            if has_ring:
+                                ring = made[1][r - r0] * inside
+                            if r < 0:
+                                core, ring = core * above, ring * above
+                            elif r >= rows:
+                                core, ring = core * below, ring * below
+                            hc[t, r + pad] = core.astype(bf16)
+                            if not last_sec:
+                                if direct(s):
+                                    hr[t, r + pad] = ring.astype(bf16)
+                                elif 0 <= r < rows:
+                                    col_n[t, 0, r] = core[:RING // 2].astype(bf16)
+                                    col_n[t, 1, r] = core[cols - RING // 2:].astype(bf16)
+                            if not final:
+                                spread(sh.at[t], rh.at[t], r, jnp.concatenate([core, ring], axis=0))
+                    if len(blocks) > 1:
+                        each(exchange_msgs(s, t, c, i), 1, t, send_sem, "start")
+                    elif not last_sec:
+                        each(msgs(s, t, c), 1, t, send_sem, "start")
 
         if s == 0:
-            for t in range(steps):
+            for t in range(1, steps):
                 each(frame_msgs(t), 0, t, frame_sem, "wait")
         if steps == 1:
             load_w(1).wait()
@@ -353,9 +383,11 @@
             scratch_shapes=[
                 pltpu.VMEM((steps, high, cols, width), bf16),
                 pltpu.VMEM((steps, 2, high, RING, width), bf16),
+                pltpu.VMEM((steps, 2, high, RING // 2, width), bf16),
                 pltpu.VMEM((steps, high, cols, width), bf16),
                 pltpu.VMEM((steps, high, RING, width), bf16),
                 pltpu.VMEM((steps, 2, rows, RING, width), bf16),
+                pltpu.VMEM((steps, 2, rows, RING // 2, width), bf16),
                 pltpu.VMEM(weight.shape[1:], bf16),
                 pltpu.VMEM(bias.shape, f32),
                 pltpu.VMEM((high, cols, 2 * width), bf16),
@@ -365,7 +397,7 @@
                 pltpu.VMEM((high * (cols + RING), 4 * width), f32),
                 pltpu.VMEM((high, cols, width), f32),
                 pltpu.VMEM((high, RING, width), f32),
-                pltpu.SemaphoreType.DMA((steps + 3,)),
+                pltpu.SemaphoreType.DMA((3 * steps + 3,)),
                 pltpu.SemaphoreType.DMA((steps, MSGS)),
                 pltpu.SemaphoreType.DMA((steps, MSGS)),
                 pltpu.SemaphoreType.DMA((steps, MSGS)),

time: 25.4 us -> 24.6 us (0.969)
  Pallas kernels: 23.8 us -> 23.1 us
    pallas_call x1, Pallas kernels: 23.8 us -> 23.1 us  [step(): pl.pallas_call(lambda *refs: body(sizes, *refs), out_shape=(jax.ShapeDtyp...]
where the time goes in v3:
time: 24.6 us; the launch traced here: 24.5 us
  Pallas kernels  23.1 us (94%)
  other arithmetic  0.8 us (3%)
  between operations  0.64 us (3%)
    pallas_call x1, Pallas kernels, step(): pl.pallas_call(lambda *refs: body(sizes, *refs), out_shape=(jax.ShapeDtyp...  23.1 us
    convert_element_type x1, other arithmetic, step(): return ((opened * jnp.tanh(cell)).astype(bf16), cell)  0.8 us

profile of v3, /device:TPU:11, one launch (start us, length us, event | category | flops | bytes accessed | tf_op | source)
XLA Modules:
  0.0 24.5 jit_solution(8849067853346234580)
XLA Ops:
  0.6 23.1 %shard_map.50 = (f32[1,16,32,128]{3,2,1,0:T(8,128)S(1)}, f32[1,16,32,128]{3,2,1,0:T(8,128)S(1)}, f32[1,16,32,128]{3,2,1,0:T(8,128)S(1)}) custom-call(bf16[3,16,32,128]{3,2,1,0:T(8,128)(2,1)} %refs_0_.1, bf16[1,9,256,512]{3,2,1,0:T(8,128)(2,1)} %refs_1_.1, f32[1,512]{1,0:T(1,128)} %refs_2_.1), custom_call_target="tpu_custom_call" | custom-call | tf_op jit(solution)/shard_map/pallas_call | solution.py:378
  23.7 0.8 %multiply_convert_fusion = (bf16[1,16,32,128]{3,2,1,0:T(8,128)(2,1)}, f32[1,16,32,128]{3,2,1,0:T(8,128)}) fusion(f32[1,16,32,128]{3,2,1,0:T(8,128)S(1)} %get-tuple-element.5, f32[1,16,32,128]{3,2,1,0:T(8,128)S(1)} %get-tuple-element.6, f32[1,16,32,128]{3,2,1,0:T(8,128)S(1)} %get-tuple-element.7), kind=kLoop, calls=%fused_computation | loop fusion | flops 196608 | bytes 1179648 | tf_op jit(solution)/shard_map/convert_element_type | solution.py:409
